TPU v7x, 256 devices: a whole 4x4x8 slice. The times are simulated.
256 devices in a mesh: ctx: 32 (over x, z), kvh: 8 (over y, core).
Axes of the slice: x: 4, y: 4, z: 8, core: 2. Of those that a mesh axis runs over, the one named last changes fastest.
Arguments:
- queries: bfloat16 [12, 16, 8192], P(None, None, 'kvh'), may hold values from -100 to 100
- keys: bfloat16 [2048, 8, 256, 128], P('ctx', 'kvh'), may hold values from -8 to 8
- values: bfloat16 [2048, 8, 256, 128], P('ctx', 'kvh'), may hold values from -6 to 6
- out_weight: bfloat16 [8192, 8192], P('kvh', 'ctx'), may hold values from -0.0625 to 0.0625
- lengths: int32 [12], replicated, may hold values from 16 to 16384, as said below
- slot_request: int32 [2048], P('ctx'), may hold values from 0 to 12, as said below
- slot_page: int32 [2048], P('ctx'), may hold values from 0 to 63, as said below
Outputs:
- projected: bfloat16 [192, 8192], P('kvh', 'ctx')
Inputs may be any that keep to these rules, and one draw needn't show every extreme that they name: `lengths`: some request has length 16 and some request has length 16384. slot_request is 12 for an empty slot; each page 0 to (lengths[r] - 1) // 256 of request r stands in exactly one slot, and no other page of it does. `slot_page`: 0 for an empty slot.
All inputs are finite; a program needn't handle non-finite values.
Results may differ from a plain program's by a relative error of at most 0.015.
Values may be sent and summed in bfloat16 or wider, within the bound.
A program may use at most 128 MiB of HBM per device.

v0:
```python
import math

import jax
import jax.numpy as jnp
from jax import lax
from jax.sharding import PartitionSpec as P

QUERY_HEADS = 64
KEY_VALUE_HEADS = 8
DRAFT_TOKENS = 16


NEGATIVE_FLOOR = -1e30
PRECISE = lax.Precision.HIGHEST


def merged(part, axis, combine):
    gathered = jax.tree.map(lambda a: lax.all_gather(a, axis), part)

    def take(source):
        return jax.tree.map(lambda a: lax.dynamic_index_in_dim(a, source, 0, False), gathered)

    return lax.fori_loop(
        1, lax.axis_size(axis), lambda source, state: combine(state, take(source)), take(0)
    )


def fold_pages(running, block_data, query_lookup_table, lengths, draft, query_group_width):
    maxima, running_totals, output_rows = running
    key_block, value_block, page_request, page_index = block_data
    requests = query_lookup_table.shape[0]
    page_len = key_block.shape[2]
    head_dim = key_block.shape[3]
    request_ids = jnp.arange(requests, dtype=jnp.int32)
    belongs = page_request[:, None] == request_ids[None, :]
    onehot = belongs.astype(jnp.float32)
    chosen = jnp.einsum(
        "br,rhqd->bhqd",
        belongs.astype(jnp.bfloat16),
        query_lookup_table,
        preferred_element_type=jnp.float32,
    ).astype(jnp.bfloat16)
    scores = jnp.einsum(
        "bhqd,bhkd->bhqk", chosen, key_block, preferred_element_type=jnp.float32
    ) * (1.0 / math.sqrt(head_dim))
    own_length = jnp.sum(jnp.where(belongs, lengths[None, :], 0), axis=1)
    draft_row = jnp.arange(query_lookup_table.shape[2], dtype=jnp.int32) // query_group_width
    query_pos = own_length[:, None] - draft + draft_row[None, :]
    key_pos = page_index[:, None] * page_len + jnp.arange(page_len, dtype=jnp.int32)[None, :]
    visible = (page_request < requests)[:, None, None] & (
        key_pos[:, None, :] <= query_pos[:, :, None]
    )
    visible = visible[:, None, :, :]
    masked = jnp.where(visible, scores, NEGATIVE_FLOOR)
    page_max = jnp.max(masked, axis=3)
    weights = jnp.where(visible, jnp.exp(masked - page_max[..., None]), 0.0)
    page_mass = jnp.sum(weights, axis=3)
    page_out = jnp.einsum(
        "bhqk,bhkd->bhqd",
        weights.astype(jnp.bfloat16),
        value_block,
        preferred_element_type=jnp.float32,
    )
    request_max = jnp.max(
        jnp.where(belongs[:, :, None, None], page_max[:, None], NEGATIVE_FLOOR), axis=0
    )
    new_maxima = jnp.maximum(maxima, request_max)
    carry_keep = jnp.exp(maxima - new_maxima)
    page_ref = jnp.einsum("br,rhq->bhq", onehot, new_maxima, precision=PRECISE)
    factor = jnp.exp(page_max - page_ref)
    running_totals = running_totals * carry_keep + jnp.einsum(
        "br,bhq->rhq", onehot, page_mass * factor, precision=PRECISE
    )
    output_rows = output_rows * carry_keep[..., None] + jnp.einsum(
        "br,bhqd->rhqd", onehot, page_out * factor[..., None], precision=PRECISE
    )
    return (new_maxima, running_totals, output_rows)


def combine(earlier, later):
    max_one, sum_one, out_one = earlier
    max_two, sum_two, out_two = later
    joined = jnp.maximum(max_one, max_two)
    scale_one = jnp.exp(max_one - joined)
    scale_two = jnp.exp(max_two - joined)
    return (
        joined,
        sum_one * scale_one + sum_two * scale_two,
        out_one * scale_one[..., None] + out_two * scale_two[..., None],
    )


def per_device(queries, keys, values, out_weight, lengths, slot_request, slot_page):
    requests = queries.shape[0]
    kv_local = keys.shape[1]
    head_dim = keys.shape[3]
    query_group_width = QUERY_HEADS // KEY_VALUE_HEADS
    query_matrix_rows = DRAFT_TOKENS * query_group_width
    query_lookup_table = (
        queries.reshape(requests, DRAFT_TOKENS, kv_local, query_group_width, head_dim)
        .transpose(0, 2, 1, 3, 4)
        .reshape(requests, kv_local, query_matrix_rows, head_dim)
    )
    slot_total = keys.shape[0]
    pages_per_block = 4
    block_total = slot_total // pages_per_block

    def visit(counter, running):
        first_slot = counter * pages_per_block
        block_data = tuple(
            (
                lax.dynamic_slice_in_dim(source, first_slot, pages_per_block, 0)
                for source in (keys, values, slot_request, slot_page)
            )
        )
        return fold_pages(
            running, block_data, query_lookup_table, lengths, DRAFT_TOKENS, query_group_width
        )

    initial_state = (
        jnp.full((requests, kv_local, query_matrix_rows), NEGATIVE_FLOOR, jnp.float32),
        jnp.zeros((requests, kv_local, query_matrix_rows), jnp.float32),
        jnp.zeros((requests, kv_local, query_matrix_rows, head_dim), jnp.float32),
    )
    maxima, running_totals, output_rows = lax.fori_loop(0, block_total, visit, initial_state)
    maxima, running_totals, output_rows = merged(
        (maxima, running_totals, output_rows), "ctx", combine
    )
    attended_output = (output_rows / running_totals[..., None]).astype(jnp.bfloat16)
    attended_output = (
        attended_output.reshape(requests, kv_local, DRAFT_TOKENS, query_group_width, head_dim)
        .transpose(0, 2, 1, 3, 4)
        .reshape(requests * DRAFT_TOKENS, kv_local * query_group_width * head_dim)
    )
    return lax.psum_scatter(
        jnp.dot(attended_output, out_weight, preferred_element_type=jnp.float32).astype(
            jnp.bfloat16
        ),
        "kvh",
        scatter_dimension=0,
        tiled=True,
    )


def solution(mesh):
    placed = (
        P(None, None, "kvh"),
        P("ctx", "kvh", None, None),
        P("ctx", "kvh", None, None),
        P("kvh", "ctx"),
        P(),
        P("ctx"),
        P("ctx"),
    )
    return jax.shard_map(
        per_device, mesh=mesh, in_specs=placed, out_specs=P("kvh", "ctx"), check_vma=False
    )
```

profile of v0, /device:TPU:1, one launch (start us, length us, event | category | flops | bytes accessed | tf_op | source)
XLA Modules:
  0.0 419.7 jit_solution(11182441481139594307)
XLA Ops:
  8.0 123.9 %while.40 = (s32[]{:T(128)}, f32[12,1,128]{2,0,1:T(8,128)S(1)}, f32[12,1,128]{2,0,1:T(8,128)S(1)}, f32[12,1,128,128]{3,0,2,1:T(8,128)S(1)}, s32[64]{0:T(128)}, /...) while((s32[]{:T(128)}, f32[12,1,128]{2,0,1:T(8,128)S(1)}, ...), condition=%wide.region_5.6_spmd.clone, body=%wide.region_0.5_spmd.clone.sunk | while | flops 80979344 | bytes 4988615 | solution.py:125
  12.9 1.3 convolution_multiply_fusion.3
  18.7 1.3 fusion.60
  20.7 1.3 convolution_multiply_fusion.3
  26.5 1.3 fusion.60
  28.4 1.3 convolution_multiply_fusion.3
  36.1 1.3 convolution_multiply_fusion.3
  42.0 1.3 fusion.60
  43.9 1.3 convolution_multiply_fusion.3
  51.6 1.3 convolution_multiply_fusion.3
  57.4 1.3 fusion.60
  59.4 1.3 convolution_multiply_fusion.3
  65.2 1.3 fusion.60
  67.1 1.3 convolution_multiply_fusion.3
  72.9 1.3 fusion.60
  74.9 1.3 convolution_multiply_fusion.3
  80.7 1.3 fusion.60
  82.6 1.3 convolution_multiply_fusion.3
  88.4 1.3 fusion.60
  90.3 1.3 convolution_multiply_fusion.3
  96.2 1.3 fusion.60
  98.1 1.3 convolution_multiply_fusion.3
  103.9 1.3 fusion.60
  105.8 1.3 convolution_multiply_fusion.3
  113.6 1.3 convolution_multiply_fusion.3
  119.4 1.3 fusion.60
  121.3 1.3 convolution_multiply_fusion.3
  129.1 1.3 convolution_multiply_fusion.3
  133.2 42.7 %all-gather.1 = f32[384,1,128]{2,1,0:T(1,128)S(1)} all-gather(f32[12,1,128]{2,1,0:T(1,128)S(1)} %copy.52), channel_id=3, replica_groups=mesh['ctx'=32,'kvh'=8] {'ctx'}, dimensions={0}, use_global_device_ids=true | all-gather | bytes 202752 | tf_op jit(solution)/shard_map/all_gather | solution.py:18
  176.0 37.4 %all-gather = f32[384,1,128]{2,1,0:T(1,128)S(1)} all-gather(f32[12,1,128]{2,1,0:T(1,128)S(1)} %copy.51), channel_id=2, replica_groups=mesh['ctx'=32,'kvh'=8] {'ctx'}, dimensions={0}, use_global_device_ids=true | all-gather | bytes 202752 | tf_op jit(solution)/shard_map/all_gather | solution.py:18
  213.4 109.1 %all-gather.5.cloned.1.call-done = f32[384,1,128,128]{3,2,1,0:T(8,128)} async-done(((f32[12,1,128,128]{3,2,1,0:T(8,128)}), f32[384,1,128,128]{3,2,1,0:T(8,128)}) %all-gather.5.cloned.1.call-update) | async-done | bytes 25165840 | tf_op jit(solution)/shard_map/all_gather | solution.py:18
  323.7 60.1 %while.39 = (s32[]{:T(128)}, f32[12,1,128]{2,1,0:T(1,128)S(1)}, f32[12,1,128]{2,1,0:T(1,128)S(1)}, f32[12,1,128,128]{3,2,1,0:T(8,128)S(1)}, f32[32,12,1,128]{3,2...) while((s32[]{:T(128)}, f32[12,1,128]{2,1,0:T(1,128)S(1)}, ...), condition=%wide.region_7.8_spmd, body=%wide.region_6.7_spmd.sunk | while | flops 599045 | bytes 2445455 | solution.py:23
  323.8 1.9 fusion.51
  325.7 1.9 fusion.51
  327.6 1.9 fusion.51
  329.6 1.9 fusion.51
  331.5 1.9 fusion.51
  333.5 1.9 fusion.51
  335.4 1.9 fusion.51
  337.3 1.9 fusion.51
  339.3 1.9 fusion.51
  341.2 1.9 fusion.51
  343.2 1.9 fusion.51
  345.1 1.9 fusion.51
  347.0 1.9 fusion.51
  349.0 1.9 fusion.51
  350.9 1.9 fusion.51
  352.8 1.9 fusion.51
  354.8 1.9 fusion.51
  356.7 1.9 fusion.51
  358.7 1.9 fusion.51
  360.6 1.9 fusion.51
  362.5 1.9 fusion.51
  364.5 1.9 fusion.51
  366.4 1.9 fusion.51
  368.4 1.9 fusion.51
  370.3 1.9 fusion.51
  372.2 1.9 fusion.51
  374.2 1.9 fusion.51
  376.1 1.9 fusion.51
  378.0 1.9 fusion.51
  380.0 1.9 fusion.51
  381.9 1.9 fusion.51
  385.2 27.6 %reduce-scatter.2.cloned.1.call-done = bf16[24,256]{1,0:T(8,128)(2,1)} async-done(((bf16[192,256]{1,0:T(8,128)(2,1)}), bf16[24,256]{1,0:T(8,128)(2,1)}) %reduce-scatter.2.cloned.1.call-update) | async-done | bytes 12304 | tf_op jit(solution)/shard_map/reduce_scatter | solution.py:135
  (376 shorter events, 94.8 us)
Async XLA Ops:
  6.5 377.7 %copy-start = (bf16[1024,256]{1,0:T(8,128)(2,1)S(1)}, bf16[1024,256]{1,0:T(8,128)(2,1)}, u32[]{:S(2)}) copy-start(bf16[1024,256]{1,0:T(8,128)(2,1)} %param.14) | copy-start | bytes 1572868
  6.5 316.0 %all-gather.5.cloned.1.call-start = ((), (), s32[]{:S(2)}) async-start(), calls=%async_computation.2 | async-start | bytes 25952256 | tf_op jit(solution)/shard_map/all_gather | solution.py:18
  133.1 279.7 %reduce-scatter.2.cloned.1.call-start = ((), (), s32[]{:S(2)}) async-start(), calls=%async_computation.1 | async-start | bytes 110592 | tf_op jit(solution)/shard_map/reduce_scatter | solution.py:135
Sparse Core Ops, SparseCore 0:
  133.3 189.2 all-gather.4
  385.3 27.4 reduce-scatter.1
where the time goes:
time: 424 us; the launch traced here: 420 us
  waiting for transfers between devices  137 us (32%)
  other arithmetic  107 us (25%)
  blocking collectives  80.1 us (19%)
  matrix products  72.8 us (17%)
  between operations  13.5 us (3%)
  local copies, waits for them, and re-layouts  7.68 us (2%)
    all_gather x1, waiting for transfers between devices, merged(): gathered = jax.tree.map(lambda a: lax.all_gather(a, axis), part)  109 us
    all_gather x2, blocking collectives, merged(): gathered = jax.tree.map(lambda a: lax.all_gather(a, axis), part)  80.1 us
    add x31, other arithmetic, combine(): out_one * scale_one[..., None] + out_two * scale_two[..., None]  57.7 us
    reduce_scatter x1, waiting for transfers between devices, per_device(): lax.psum_scatter(jnp.dot(attended_output, out_weight, preferred_element_t...  27.6 us
    dot_general x16, matrix products, fold_pages(): jnp.einsum('bhqk,bhkd->bhqd', weights.astype(jnp.bfloat16), value_block,...  20.8 us
    dot_general x16, matrix products, fold_pages(): jnp.einsum('bhqd,bhkd->bhqk', chosen, key_block, preferred_element_type=j...  20.5 us
    dot_general x16, matrix products, fold_pages(): jnp.einsum('br,bhqd->rhqd', onehot, page_out * factor[..., None], precisi...  19 us
    reduce_sum x16, other arithmetic, fold_pages(): own_length = jnp.sum(jnp.where(belongs, lengths[None, :], 0), axis=1)  13.4 us
  transfers between devices with their start and end apart: 2, of which 2 were waited for; matrix products, arithmetic and copies ran while one was open for 0% of the time, Pallas kernels for 0%

commit v1 on v0

v1 whole, which is shorter than its diff:
```python
import functools
import math

import jax
import jax.numpy as jnp
from jax import lax
from jax.experimental import pallas as pl
from jax.experimental.pallas import tpu as pltpu
from jax.sharding import PartitionSpec as P

QUERY_HEADS = 64
KEY_VALUE_HEADS = 8
DRAFT_TOKENS = 16
GROUP = QUERY_HEADS // KEY_VALUE_HEADS

MASKED = -1e30
FLOOR = -0.5e30
MESH = pl.DeviceIdType.MESH


def attend(
    request_ref, page_ref, length_ref, q_ref, k_hbm, v_hbm, o_ref, stat_ref,
    q_rows, k_buf, v_buf, s_buf, lane_max, row_max, mass, acc, k_sem, v_sem,
):
    slots, page_tokens, head_dim = k_buf.shape
    requests = q_ref.shape[0]
    rows = q_rows.shape[1]
    per_owner = o_ref.shape[1]
    block = slots // k_sem.shape[0]
    scale2 = math.log2(math.e) / math.sqrt(head_dim)

    for b in range(slots // block):
        part = pl.ds(b * block, block)
        pltpu.make_async_copy(k_hbm.at[part, 0], k_buf.at[part], k_sem.at[b]).start()
    for b in range(slots // block):
        part = pl.ds(b * block, block)
        pltpu.make_async_copy(v_hbm.at[part, 0], v_buf.at[part], v_sem.at[b]).start()

    for r in range(requests):
        for h in range(GROUP):
            q_rows[r, h * DRAFT_TOKENS:(h + 1) * DRAFT_TOKENS, :] = q_ref[r, :, h * head_dim:(h + 1) * head_dim]
    lane_max[...] = jnp.full(lane_max.shape, FLOOR, jnp.float32)
    mass[...] = jnp.zeros(mass.shape, jnp.float32)
    acc[...] = jnp.zeros(acc.shape, jnp.float32)
    ahead = lax.broadcasted_iota(jnp.int32, (DRAFT_TOKENS, page_tokens), 1) - lax.broadcasted_iota(
        jnp.int32, (DRAFT_TOKENS, page_tokens), 0
    )

    def score(b, carry):
        part = pl.ds(b * block, block)
        pltpu.make_async_copy(k_hbm.at[part, 0], k_buf.at[part], k_sem.at[b]).wait()
        for u in range(block):
            slot = b * block + u
            r = request_ref[slot]
            known = jnp.minimum(r, requests - 1)
            limit = length_ref[known] - DRAFT_TOKENS - page_ref[slot] * page_tokens
            s = lax.dot_general(
                q_rows[known], k_buf[slot], (((1,), (1,)), ((), ())), preferred_element_type=jnp.float32
            )
            visible = ahead <= limit
            for h in range(GROUP):
                at = slice(h * DRAFT_TOKENS, (h + 1) * DRAFT_TOKENS)
                masked = jnp.where(visible, s[at], MASKED)
                s_buf[slot, at, :] = masked
                folded = jnp.maximum(masked[:, :head_dim], masked[:, head_dim:])
                lane_max[r, at, :] = jnp.maximum(lane_max[r, at, :], folded)
        return carry

    lax.fori_loop(0, slots // block, score, 0)

    for r in range(requests):
        row_max[r] = jnp.broadcast_to(jnp.max(lane_max[r], axis=1, keepdims=True), (rows, head_dim))
    row_max[requests] = jnp.zeros((rows, head_dim), jnp.float32)

    def weigh(b, carry):
        part = pl.ds(b * block, block)
        pltpu.make_async_copy(v_hbm.at[part, 0], v_buf.at[part], v_sem.at[b]).wait()
        for u in range(block):
            slot = b * block + u
            r = request_ref[slot]
            reference = row_max[r]
            left = jnp.exp2((s_buf[slot, :, :head_dim] - reference) * scale2)
            right = jnp.exp2((s_buf[slot, :, head_dim:] - reference) * scale2)
            mass[r] += left + right
            weights = jnp.concatenate([left, right], axis=1).astype(jnp.bfloat16)
            acc[r] += jnp.dot(weights, v_buf[slot], preferred_element_type=jnp.float32)
        return carry

    lax.fori_loop(0, slots // block, weigh, 0)

    lane = lax.broadcasted_iota(jnp.int32, (rows, head_dim), 1)
    row = lax.broadcasted_iota(jnp.int32, (rows, head_dim), 0)
    diagonal = lane % DRAFT_TOKENS == row % DRAFT_TOKENS
    piece = lane // DRAFT_TOKENS
    for a in range(requests // per_owner):
        packed = jnp.zeros((rows, head_dim), jnp.float32)
        for i in range(per_owner):
            r = a * per_owner + i
            total = jnp.sum(mass[r], axis=1, keepdims=True)
            packed = jnp.where(piece == i, row_max[r], packed)
            packed = jnp.where(piece == per_owner + i, jnp.broadcast_to(total, (rows, head_dim)), packed)
        packed = jnp.where(diagonal, packed, 0.0)
        for h in range(GROUP):
            at = slice(h * DRAFT_TOKENS, (h + 1) * DRAFT_TOKENS)
            stat_ref[a * GROUP + h] = jnp.sum(packed[at], axis=0, keepdims=True)
            for i in range(per_owner):
                o_ref[a * GROUP + h, i] = acc[a * per_owner + i, at, :].astype(jnp.bfloat16)


def exchange(
    n_ctx, n_kvh, o_ref, stat_ref, w_ref, out_ref,
    o_in, stat_in, att, share, o_send, o_recv, t_send, t_recv, a_send, a_recv, p_send, p_recv,
):
    c = lax.axis_index("ctx")
    k = lax.axis_index("kvh")
    per_owner, tokens, head_dim = o_ref.shape[1:]
    scale2 = math.log2(math.e) / math.sqrt(head_dim)

    def ctx_peer(i):
        return lax.rem(c + i, n_ctx)

    def kvh_peer(i):
        return lax.rem(k + i, n_kvh)

    barrier = pltpu.get_barrier_semaphore()

    def greet_ctx(i, carry):
        pl.semaphore_signal(barrier, inc=1, device_id=(ctx_peer(i), k), device_id_type=MESH)
        return carry

    def greet_kvh(i, carry):
        pl.semaphore_signal(barrier, inc=1, device_id=(c, kvh_peer(i)), device_id_type=MESH)
        return carry

    lax.fori_loop(1, n_ctx, greet_ctx, 0)
    lax.fori_loop(1, n_kvh, greet_kvh, 0)
    pl.semaphore_wait(barrier, n_ctx + n_kvh - 2)

    def stat_copy(i):
        return pltpu.make_async_remote_copy(
            src_ref=stat_ref.at[ctx_peer(i)], dst_ref=stat_in.at[c],
            send_sem=t_send.at[i], recv_sem=t_recv.at[i],
            device_id=(ctx_peer(i), k), device_id_type=MESH,
        )

    def o_copy(i):
        return pltpu.make_async_remote_copy(
            src_ref=o_ref.at[ctx_peer(i)], dst_ref=o_in.at[c],
            send_sem=o_send.at[i], recv_sem=o_recv.at[i],
            device_id=(ctx_peer(i), k), device_id_type=MESH,
        )

    def att_copy(i):
        return pltpu.make_async_remote_copy(
            src_ref=att.at[c], dst_ref=att.at[c],
            send_sem=a_send.at[i], recv_sem=a_recv.at[i],
            device_id=(ctx_peer(i), k), device_id_type=MESH,
        )

    def share_copy(i):
        return pltpu.make_async_remote_copy(
            src_ref=share.at[kvh_peer(i)], dst_ref=out_ref.at[k],
            send_sem=p_send.at[i], recv_sem=p_recv.at[i],
            device_id=(c, kvh_peer(i)), device_id_type=MESH,
        )

    def start_partials(i, carry):
        stat_copy(i).start()
        o_copy(i).start()
        return carry

    lax.fori_loop(1, n_ctx, start_partials, 0)
    stat_in[c] = stat_ref[c]
    o_in[c] = o_ref[c]

    def wait_stats(i, carry):
        stat_copy(i).wait_recv()
        return carry

    def wait_partials(i, carry):
        o_copy(i).wait_recv()
        return carry

    lax.fori_loop(1, n_ctx, wait_stats, 0)
    stats = stat_in[...].reshape(n_ctx, head_dim)
    span = per_owner * tokens
    joined = jnp.max(stats, axis=0, keepdims=True)
    factor = jnp.exp2((stats - joined) * scale2)
    masses = pltpu.roll(stats, head_dim - span, 1)
    lane = lax.broadcasted_iota(jnp.int32, stats.shape, 1)
    factor = jnp.where(lane < span, factor, 0.0)
    total = jnp.sum(factor * masses, axis=0, keepdims=True)
    total = jnp.where(lane[:1] < span, total, 1.0)
    factor = (factor / total).T
    lax.fori_loop(1, n_ctx, wait_partials, 0)
    attended = jnp.zeros((span, head_dim), jnp.float32)
    for s in range(n_ctx):
        attended += factor[:span, s:s + 1] * o_in[s].reshape(span, head_dim).astype(jnp.float32)
    att[c] = attended.astype(jnp.bfloat16).reshape(per_owner, tokens, head_dim)

    def start_att(i, carry):
        att_copy(i).start()
        return carry

    def wait_att(i, carry):
        att_copy(i).wait_recv()
        return carry

    lax.fori_loop(1, n_ctx, start_att, 0)
    lax.fori_loop(1, n_ctx, wait_att, 0)

    heads = w_ref.shape[0] // head_dim
    groups = n_ctx // heads
    operand = jnp.concatenate(
        [
            jnp.concatenate([att[a * heads + h].reshape(span, head_dim) for a in range(groups)], axis=0)
            for h in range(heads)
        ],
        axis=1,
    )
    product = jnp.dot(operand, w_ref[...], preferred_element_type=jnp.float32).astype(jnp.bfloat16)
    part = share.shape[1]
    for d in range(n_kvh):
        share[d] = product[d * part:(d + 1) * part]

    def start_share(i, carry):
        share_copy(i).start()
        return carry

    def finish_share(i, carry):
        share_copy(i).wait()
        return carry

    def finish_ctx(i, carry):
        stat_copy(i).wait_send()
        o_copy(i).wait_send()
        att_copy(i).wait_send()
        return carry

    lax.fori_loop(1, n_kvh, start_share, 0)
    out_ref[k] = share[k]
    lax.fori_loop(1, n_ctx, finish_ctx, 0)
    lax.fori_loop(1, n_kvh, finish_share, 0)


def per_device(n_ctx, n_kvh, queries, keys, values, out_weight, lengths, slot_request, slot_page):
    requests = queries.shape[0]
    slots, _, page_tokens, head_dim = keys.shape
    rows = DRAFT_TOKENS * GROUP
    per_owner = requests * GROUP // n_ctx
    owned = (n_ctx, per_owner, DRAFT_TOKENS, head_dim)
    smem = pl.BlockSpec(memory_space=pltpu.SMEM)
    vmem = pl.BlockSpec(memory_space=pltpu.VMEM)
    hbm = pl.BlockSpec(memory_space=pl.ANY)
    blocks = slots // 4
    partial, stats = pl.pallas_call(
        attend,
        out_shape=(
            jax.ShapeDtypeStruct(owned, jnp.bfloat16),
            jax.ShapeDtypeStruct((n_ctx, 1, head_dim), jnp.float32),
        ),
        in_specs=[smem, smem, smem, vmem, hbm, hbm],
        out_specs=(vmem, vmem),
        scratch_shapes=[
            pltpu.VMEM((requests, rows, head_dim), jnp.bfloat16),
            pltpu.VMEM((slots, page_tokens, head_dim), jnp.bfloat16),
            pltpu.VMEM((slots, page_tokens, head_dim), jnp.bfloat16),
            pltpu.VMEM((slots, rows, page_tokens), jnp.float32),
            pltpu.VMEM((requests + 1, rows, head_dim), jnp.float32),
            pltpu.VMEM((requests + 1, rows, head_dim), jnp.float32),
            pltpu.VMEM((requests + 1, rows, head_dim), jnp.float32),
            pltpu.VMEM((requests + 1, rows, head_dim), jnp.float32),
            pltpu.SemaphoreType.DMA((blocks,)),
            pltpu.SemaphoreType.DMA((blocks,)),
        ],
        compiler_params=pltpu.CompilerParams(vmem_limit_bytes=40 << 20),
        name="attend",
    )(slot_request, slot_page, lengths, queries, keys, values)

    total_rows = requests * DRAFT_TOKENS
    columns = out_weight.shape[1]
    shares = pl.pallas_call(
        functools.partial(exchange, n_ctx, n_kvh),
        out_shape=jax.ShapeDtypeStruct((n_kvh, total_rows // n_kvh, columns), jnp.bfloat16),
        in_specs=[vmem, vmem, vmem],
        out_specs=vmem,
        scratch_shapes=[
            pltpu.VMEM(owned, jnp.bfloat16),
            pltpu.VMEM((n_ctx, 1, head_dim), jnp.float32),
            pltpu.VMEM(owned, jnp.bfloat16),
            pltpu.VMEM((n_kvh, total_rows // n_kvh, columns), jnp.bfloat16),
        ]
        + [pltpu.SemaphoreType.DMA((n_ctx,))] * 6
        + [pltpu.SemaphoreType.DMA((n_kvh,))] * 2,
        compiler_params=pltpu.CompilerParams(
            collective_id=0, has_side_effects=True, vmem_limit_bytes=32 << 20
        ),
        name="exchange",
    )(partial, stats, out_weight)
    return jnp.sum(shares.astype(jnp.float32), axis=0).astype(jnp.bfloat16)


def solution(mesh):
    placed = (
        P(None, None, "kvh"),
        P("ctx", "kvh", None, None),
        P("ctx", "kvh", None, None),
        P("kvh", "ctx"),
        P(),
        P("ctx"),
        P("ctx"),
    )
    return jax.shard_map(
        functools.partial(per_device, mesh.shape["ctx"], mesh.shape["kvh"]),
        mesh=mesh, in_specs=placed, out_specs=P("kvh", "ctx"), check_vma=False,
    )
```

time: 424 us -> 58.9 us (0.14)
  waiting for transfers between devices: 137 us -> 0 us
  other arithmetic: 107 us -> 0.62 us
  blocking collectives: 80.1 us -> 0 us
  matrix products: 72.8 us -> 0 us
  Pallas kernels: 0 us -> 50.7 us
  between operations: 13.5 us -> 0.03 us
    all_gather x1 -> x0, waiting for transfers between devices: 109 us -> none  [merged(): gathered = jax.tree.map(lambda a: lax.all_gather(a, axis), part)]
    all_gather x2 -> x0, blocking collectives: 80.1 us -> none  [merged(): gathered = jax.tree.map(lambda a: lax.all_gather(a, axis), part)]
    dot_general x97 -> x0, matrix products: 72.8 us -> none  [the longest x16 20.8 us: fold_pages(): jnp.einsum('bhqk,bhkd->bhqd', weights.astype(jnp.bfloat16), value_block,...]
    add x94 -> x0, other arithmetic: 61.3 us -> none  [the longest x31 57.7 us: combine(): out_one * scale_one[..., None] + out_two * scale_two[..., None]]
    pallas_call x0 -> x2, Pallas kernels: none -> 50.7 us  [the longest x1 40.6 us: per_device(): pl.pallas_call(functools.partial(exchange, n_ctx, n_kvh), out_shape=jax.S...]
    reduce_scatter x1 -> x0, waiting for transfers between devices: 27.6 us -> none  [per_device(): lax.psum_scatter(jnp.dot(attended_output, out_weight, preferred_element_t...]
    reduce_sum x32 -> x1, other arithmetic: 18.8 us -> 0.62 us  [per_device(): return jnp.sum(shares.astype(jnp.float32), axis=0).astype(jnp.bfloat16)]
    mul x32 -> x0, other arithmetic: 11.9 us -> none  [the longest x16 11.7 us: fold_pages(): page_index[:, None] * page_len]
  transfers between devices with their start and end apart: 2 -> 0, of which waited for: 2 -> 0; matrix products, arithmetic and copies ran while one was open for 0% -> 0% of each run, Pallas kernels for 0% -> 0%
where the time goes in v1:
time: 58.9 us; the launch traced here: 58.7 us
  Pallas kernels  50.7 us (86%)
  local copies, waits for them, and re-layouts  7.34 us (12%)
  other arithmetic  0.62 us (1%)
    pallas_call x1, Pallas kernels, per_device(): pl.pallas_call(functools.partial(exchange, n_ctx, n_kvh), out_shape=jax.S...  40.6 us
    pallas_call x1, Pallas kernels, per_device(): pl.pallas_call(attend, out_shape=(jax.ShapeDtypeStruct(owned, jnp.bfloat1...  10.1 us
    unnamed x14, local copies, waits for them, and re-layouts  7.34 us

profile of v1, /device:TPU:1, one launch (start us, length us, event | category | flops | bytes accessed | tf_op | source)
XLA Modules:
  0.0 58.7 jit_solution(13212709143234302127)
XLA Ops:
  0.0 0.0 copy-start
  0.0 2.2 %copy-done = bf16[64,1,256,128]{3,2,1,0:T(8,128)(2,1)S(1)} copy-done((bf16[64,1,256,128]{3,2,1,0:T(8,128)(2,1)S(1)}, bf16[64,1,256,128]{3,2,1,0:T(8,128)(2,1)}, u32[]{:S(2)}) %copy-start) | copy-done | bytes 4194328
  2.2 0.0 copy-start.1
  2.2 2.2 %copy-done.1 = bf16[64,1,256,128]{3,2,1,0:T(8,128)(2,1)S(1)} copy-done((bf16[64,1,256,128]{3,2,1,0:T(8,128)(2,1)S(1)}, bf16[64,1,256,128]{3,2,1,0:T(8,128)(2,1)}, u32[]{:S(2)}) %copy-start.1) | copy-done | bytes 4194328
  4.4 0.0 copy-start.3
  4.4 1.0 %copy-done.3 = bf16[12,16,1024]{2,1,0:T(8,128)(2,1)S(1)} copy-done((bf16[12,16,1024]{2,1,0:T(8,128)(2,1)S(1)}, bf16[12,16,1024]{2,1,0:T(8,128)(2,1)}, u32[]{:S(2)}) %copy-start.3) | copy-done | bytes 393240
  5.4 0.0 copy-start.4
  5.4 0.7 %copy-done.4 = s32[64]{0:T(128)S(1)} copy-done((s32[64]{0:T(128)S(1)}, s32[64]{0:T(128)}, u32[]{:S(2)}) %copy-start.4) | copy-done | bytes 280
  6.0 0.0 copy-start.5
  6.0 0.7 %copy-done.5 = s32[64]{0:T(128)S(1)} copy-done((s32[64]{0:T(128)S(1)}, s32[64]{0:T(128)}, u32[]{:S(2)}) %copy-start.5) | copy-done | bytes 280
  6.7 0.0 copy-start.6
  6.7 0.7 %copy-done.6 = s32[12]{0:T(128)S(1)} copy-done((s32[12]{0:T(128)S(1)}, s32[12]{0:T(128)}, u32[]{:S(2)}) %copy-start.6) | copy-done | bytes 72
  7.3 0.0 copy-start.2
  7.3 10.1 %attend.1 = (bf16[32,3,16,128]{3,2,1,0:T(8,128)(2,1)S(1)}, f32[32,1,128]{2,1,0:T(1,128)S(1)}) custom-call(s32[64]{0:T(128)S(1)} %copy-done.4, s32[64]{0:T(128)S(1)} %copy-done.5, s32[12]{0:T(128)S(1)} %copy-done.6, bf16[12,16,1024]{2,1,0:T(8,128)(2,1)S(1)} %copy-done.3, bf16[64,1,256,128]{3,2,1,0:T(8,128)(2,1)S(1)} %copy-done, ...), custom_call_target="tpu_custom_call" | custom-call | tf_op jit(solution)/shard_map/attend/pallas_call | solution.py:256
  17.4 0.0 copy-done.2
  17.4 40.6 %exchange.1 = bf16[8,24,256]{2,1,0:T(8,128)(2,1)S(1)} custom-call(bf16[32,3,16,128]{3,2,1,0:T(8,128)(2,1)S(1)} %get-tuple-element.7.o_ref, f32[32,1,128]{2,1,0:T(1,128)S(1)} %get-tuple-element.8.stat_ref, bf16[1024,256]{1,0:T(8,128)(2,1)S(1)} %copy-done.2), custom_call_target="tpu_custom_call" | custom-call | tf_op jit(solution)/shard_map/exchange/pallas_call | solution.py:282
  58.1 0.6 %reduce_sum.12 = bf16[24,256]{1,0:T(8,128)(2,1)} reduce(bf16[8,24,256]{2,1,0:T(8,128)(2,1)S(1)} %exchange.1, bf16[]{:T(256)} %constant.2.clone.1), dimensions={0}, to_apply=%region_0.0 | reduce | flops 43008 | bytes 110594 | tf_op jit(solution)/shard_map/reduce_sum | solution.py:300
Async XLA Ops:
  0.0 2.2 %copy-start = (bf16[64,1,256,128]{3,2,1,0:T(8,128)(2,1)S(1)}, bf16[64,1,256,128]{3,2,1,0:T(8,128)(2,1)}, u32[]{:S(2)}) copy-start(bf16[64,1,256,128]{3,2,1,0:T(8,128)(2,1)} %k_hbm.1) | copy-start | bytes 12582916
  2.2 2.2 %copy-start.1 = (bf16[64,1,256,128]{3,2,1,0:T(8,128)(2,1)S(1)}, bf16[64,1,256,128]{3,2,1,0:T(8,128)(2,1)}, u32[]{:S(2)}) copy-start(bf16[64,1,256,128]{3,2,1,0:T(8,128)(2,1)} %v_hbm.1) | copy-start | bytes 12582916
  4.4 1.0 %copy-start.3 = (bf16[12,16,1024]{2,1,0:T(8,128)(2,1)S(1)}, bf16[12,16,1024]{2,1,0:T(8,128)(2,1)}, u32[]{:S(2)}) copy-start(bf16[12,16,1024]{2,1,0:T(8,128)(2,1)} %q_ref.1) | copy-start | bytes 1179652
  5.4 0.7 %copy-start.4 = (s32[64]{0:T(128)S(1)}, s32[64]{0:T(128)}, u32[]{:S(2)}) copy-start(s32[64]{0:T(128)} %request_ref.1) | copy-start | bytes 772
  6.0 0.7 %copy-start.5 = (s32[64]{0:T(128)S(1)}, s32[64]{0:T(128)}, u32[]{:S(2)}) copy-start(s32[64]{0:T(128)} %page_ref.1) | copy-start | bytes 772
  6.7 0.7 %copy-start.6 = (s32[12]{0:T(128)S(1)}, s32[12]{0:T(128)}, u32[]{:S(2)}) copy-start(s32[12]{0:T(128)} %length_ref.1) | copy-start | bytes 148
  7.3 10.1 %copy-start.2 = (bf16[1024,256]{1,0:T(8,128)(2,1)S(1)}, bf16[1024,256]{1,0:T(8,128)(2,1)}, u32[]{:S(2)}) copy-start(bf16[1024,256]{1,0:T(8,128)(2,1)} %w_ref.1) | copy-start | bytes 1572868

commit v2 on v1

v2 whole, which is shorter than its diff:
```python
import functools
import math

import jax
import jax.numpy as jnp
from jax import lax
from jax.experimental import pallas as pl
from jax.experimental.pallas import tpu as pltpu
from jax.sharding import PartitionSpec as P

QUERY_HEADS = 64
KEY_VALUE_HEADS = 8
DRAFT_TOKENS = 16
GROUP = QUERY_HEADS // KEY_VALUE_HEADS

MASKED = -1e30
FLOOR = -0.5e30
MESH = pl.DeviceIdType.MESH


def step(
    n_ctx, n_kvh, block,
    request_hbm, page_hbm, length_hbm, q_hbm, k_hbm, v_hbm, w_hbm, out_ref,
    request_ref, page_ref, length_ref, before_ref, last_ref,
    q_in, q_rows, k_buf, v_buf, w_buf, s_buf, lane_max, row_max, mass, acc,
    o_out, stat_out, o_in, stat_in, att, share,
    small_sem, k_sem, v_sem, o_send, o_recv, t_send, t_recv, z_send, z_recv, x_send, x_recv, p_send, p_recv,
):
    c = lax.axis_index("ctx")
    k = lax.axis_index("kvh")
    slots, page_tokens, head_dim = k_buf.shape
    requests, rows = q_rows.shape[:2]
    per_owner, tokens = o_out.shape[1:3]
    heads = rows // tokens
    groups = n_ctx // heads
    blocks = slots // block
    scale2 = math.log2(math.e) / math.sqrt(head_dim)
    x, z = c // heads, lax.rem(c, heads)

    def fetch(source, target, sem):
        return pltpu.make_async_copy(source, target, sem)

    def k_copy(b):
        part = pl.ds(b * block, block)
        return fetch(k_hbm.at[part, 0], k_buf.at[part], k_sem.at[b])

    def v_copy(b):
        part = pl.ds(b * block, block)
        return fetch(v_hbm.at[part, 0], v_buf.at[part], v_sem.at[b])

    first = [
        fetch(request_hbm, request_ref, small_sem.at[0]),
        fetch(page_hbm, page_ref, small_sem.at[1]),
        fetch(length_hbm, length_ref, small_sem.at[2]),
        fetch(q_hbm, q_in, small_sem.at[3]),
    ]
    w_copy = fetch(w_hbm, w_buf, small_sem.at[4])
    for copy in first:
        copy.start()
    for b in range(blocks):
        k_copy(b).start()
    for b in range(blocks):
        v_copy(b).start()
    w_copy.start()

    def ctx_device(j, i):
        return lax.rem(x + j, groups) * heads + lax.rem(z + i, heads)

    def kvh_device(i):
        return lax.rem(k + i, n_kvh)

    barrier = pltpu.get_barrier_semaphore()

    def greet_ctx(i, carry):
        pl.semaphore_signal(barrier, inc=1, device_id=(lax.rem(c + i, n_ctx), k), device_id_type=MESH)
        return carry

    def greet_kvh(i, carry):
        pl.semaphore_signal(barrier, inc=1, device_id=(c, kvh_device(i)), device_id_type=MESH)
        return carry

    lax.fori_loop(1, n_ctx, greet_ctx, 0)
    lax.fori_loop(1, n_kvh, greet_kvh, 0)

    lane_max[slots] = jnp.full((rows, head_dim), FLOOR, jnp.float32)
    mass[slots] = jnp.zeros((rows, head_dim), jnp.float32)
    acc[slots] = jnp.zeros((rows, head_dim), jnp.float32)
    ahead = lax.broadcasted_iota(jnp.int32, (tokens, page_tokens), 1) - lax.broadcasted_iota(
        jnp.int32, (tokens, page_tokens), 0
    )
    for copy in first:
        copy.wait()
    for r in range(requests):
        for h in range(heads):
            q_rows[r, h * tokens:(h + 1) * tokens, :] = q_in[r, :, h * head_dim:(h + 1) * head_dim]

    def score(b, last):
        k_copy(b).wait()
        for u in range(block):
            slot = b * block + u
            r = request_ref[slot]
            known = jnp.minimum(r, requests - 1)
            limit = length_ref[known] - tokens - page_ref[slot] * page_tokens
            limit = jnp.where(r < requests, limit, -page_tokens)
            before = jnp.int32(slots)
            for n in range(requests):
                before = jnp.where(r == n, last[n], before)
            last = tuple(jnp.where(r == n, slot, last[n]) for n in range(requests))
            before_ref[slot] = before
            s = lax.dot_general(
                q_rows[known], k_buf[slot], (((1,), (1,)), ((), ())), preferred_element_type=jnp.float32
            )
            visible = ahead <= limit
            for h in range(heads):
                at = slice(h * tokens, (h + 1) * tokens)
                masked = jnp.where(visible, s[at], MASKED)
                s_buf[slot, at, :] = masked
                folded = jnp.maximum(masked[:, :head_dim], masked[:, head_dim:])
                lane_max[slot, at, :] = jnp.maximum(lane_max[before, at, :], folded)
        return last

    last = lax.fori_loop(0, blocks, score, (jnp.int32(slots),) * requests)

    for r in range(requests):
        last_ref[r] = last[r]
        row_max[r] = jnp.broadcast_to(jnp.max(lane_max[last[r]], axis=1, keepdims=True), (rows, head_dim))
    row_max[requests] = jnp.zeros((rows, head_dim), jnp.float32)

    def weigh(b, carry):
        v_copy(b).wait()
        for u in range(block):
            slot = b * block + u
            before = before_ref[slot]
            reference = row_max[request_ref[slot]]
            left = jnp.exp2((s_buf[slot, :, :head_dim] - reference) * scale2)
            right = jnp.exp2((s_buf[slot, :, head_dim:] - reference) * scale2)
            mass[slot] = mass[before] + (left + right)
            weights = jnp.concatenate([left, right], axis=1).astype(jnp.bfloat16)
            acc[slot] = acc[before] + jnp.dot(weights, v_buf[slot], preferred_element_type=jnp.float32)
        return carry

    lax.fori_loop(0, blocks, weigh, 0)

    def stat_copy(j, i):
        device, n = ctx_device(j, i), j * heads + i
        return pltpu.make_async_remote_copy(
            src_ref=stat_out.at[device], dst_ref=stat_in.at[c], send_sem=t_send.at[n], recv_sem=t_recv.at[n],
            device_id=(device, k), device_id_type=MESH,
        )

    def o_copy(j, i):
        device, n = ctx_device(j, i), j * heads + i
        return pltpu.make_async_remote_copy(
            src_ref=o_out.at[device], dst_ref=o_in.at[c], send_sem=o_send.at[n], recv_sem=o_recv.at[n],
            device_id=(device, k), device_id_type=MESH,
        )

    def z_copy(i):
        return pltpu.make_async_remote_copy(
            src_ref=att.at[c], dst_ref=att.at[c], send_sem=z_send.at[i], recv_sem=z_recv.at[i],
            device_id=(ctx_device(0, i), k), device_id_type=MESH,
        )

    def x_copy(j, i):
        source, n = x * heads + lax.rem(z + heads - i, heads), j * heads + i
        return pltpu.make_async_remote_copy(
            src_ref=att.at[source], dst_ref=att.at[source], send_sem=x_send.at[n], recv_sem=x_recv.at[n],
            device_id=(ctx_device(j, 0), k), device_id_type=MESH,
        )

    def share_copy(i):
        return pltpu.make_async_remote_copy(
            src_ref=share.at[kvh_device(i)], dst_ref=out_ref.at[k], send_sem=p_send.at[i], recv_sem=p_recv.at[i],
            device_id=(c, kvh_device(i)), device_id_type=MESH,
        )

    pl.semaphore_wait(barrier, n_ctx + n_kvh - 2)

    lane = lax.broadcasted_iota(jnp.int32, (rows, head_dim), 1)
    row = lax.broadcasted_iota(jnp.int32, (rows, head_dim), 0)
    diagonal = lane % tokens == row % tokens
    piece = lane // tokens

    def hand_out(n, carry):
        j = groups - 1 - n
        a = lax.rem(x + j, groups)
        packed = jnp.zeros((rows, head_dim), jnp.float32)
        for i in range(per_owner):
            r = a * per_owner + i
            entry = last_ref[r]
            total = jnp.sum(mass[entry], axis=1, keepdims=True)
            packed = jnp.where(piece == i, row_max[r], packed)
            packed = jnp.where(piece == per_owner + i, jnp.broadcast_to(total, (rows, head_dim)), packed)
            for h in range(heads):
                at = slice(h * tokens, (h + 1) * tokens)
                o_out[a * heads + h, i] = acc[entry, at, :].astype(jnp.bfloat16)
        packed = jnp.where(diagonal, packed, 0.0)
        for h in range(heads):
            at = slice(h * tokens, (h + 1) * tokens)
            stat_out[a * heads + h] = jnp.sum(packed[at], axis=0, keepdims=True)

        def start(i, inner):
            stat_copy(j, i).start()
            o_copy(j, i).start()
            return inner

        lax.fori_loop(jnp.where(j == 0, 1, 0), heads, start, 0)
        return carry

    lax.fori_loop(0, groups, hand_out, 0)
    stat_in[c] = stat_out[c]
    o_in[c] = o_out[c]

    def each_ctx(act):
        def visit(n, carry):
            act(n // heads, lax.rem(n, heads))
            return carry

        lax.fori_loop(1, n_ctx, visit, 0)

    each_ctx(lambda j, i: stat_copy(j, i).wait_recv())
    stats = stat_in[...].reshape(n_ctx, head_dim)
    span = per_owner * tokens
    joined = jnp.max(stats, axis=0, keepdims=True)
    factor = jnp.exp2((stats - joined) * scale2)
    masses = pltpu.roll(stats, head_dim - span, 1)
    column = lax.broadcasted_iota(jnp.int32, stats.shape, 1)
    factor = jnp.where(column < span, factor, 0.0)
    total = jnp.sum(factor * masses, axis=0, keepdims=True)
    total = jnp.where(column[:1] < span, total, 1.0)
    factor = (factor / total).T
    each_ctx(lambda j, i: o_copy(j, i).wait_recv())
    attended = jnp.zeros((span, head_dim), jnp.float32)
    for s in range(n_ctx):
        attended += factor[:span, s:s + 1] * o_in[s].reshape(span, head_dim).astype(jnp.float32)
    att[c] = attended.astype(jnp.bfloat16).reshape(per_owner, tokens, head_dim)

    near_first = [i for pair in zip(range(1, heads // 2), range(heads - 1, heads // 2, -1)) for i in pair] + [heads // 2]
    beside = [1, groups - 1] + list(range(2, groups - 1))
    for i in near_first:
        z_copy(i).start()
    for j in beside:
        x_copy(j, 0).start()
    for i in near_first:
        z_copy(i).wait_recv()
        for j in beside:
            x_copy(j, i).start()
    for i in [0] + near_first:
        for j in beside:
            x_copy(j, i).wait_recv()

    w_copy.wait()
    operand = jnp.concatenate(
        [
            jnp.concatenate([att[a * heads + h].reshape(span, head_dim) for a in range(groups)], axis=0)
            for h in range(heads)
        ],
        axis=1,
    )
    product = jnp.dot(operand, w_buf[...], preferred_element_type=jnp.float32).astype(jnp.bfloat16)
    part = share.shape[1]
    for d in range(n_kvh):
        share[d] = product[d * part:(d + 1) * part]

    def start_share(i, carry):
        share_copy(i).start()
        return carry

    def finish_share(i, carry):
        share_copy(i).wait()
        return carry

    lax.fori_loop(1, n_kvh, start_share, 0)
    out_ref[k] = share[k]

    def settle(j, i):
        stat_copy(j, i).wait_send()
        o_copy(j, i).wait_send()

    each_ctx(settle)
    for i in near_first:
        z_copy(i).wait_send()
    for i in [0] + near_first:
        for j in beside:
            x_copy(j, i).wait_send()
    lax.fori_loop(1, n_kvh, finish_share, 0)


def per_device(n_ctx, n_kvh, queries, keys, values, out_weight, lengths, slot_request, slot_page):
    requests = queries.shape[0]
    slots, _, page_tokens, head_dim = keys.shape
    rows = DRAFT_TOKENS * GROUP
    per_owner = requests * GROUP // n_ctx
    owned = (n_ctx, per_owner, DRAFT_TOKENS, head_dim)
    total_rows = requests * DRAFT_TOKENS
    columns = out_weight.shape[1]
    block = 4
    blocks = slots // block
    shared = (n_kvh, total_rows // n_kvh, columns)
    shares = pl.pallas_call(
        functools.partial(step, n_ctx, n_kvh, block),
        out_shape=jax.ShapeDtypeStruct(shared, jnp.bfloat16),
        in_specs=[pl.BlockSpec(memory_space=pltpu.HBM)] * 7,
        out_specs=pl.BlockSpec(memory_space=pltpu.VMEM),
        scratch_shapes=[
            pltpu.SMEM((slots,), jnp.int32),
            pltpu.SMEM((slots,), jnp.int32),
            pltpu.SMEM((requests,), jnp.int32),
            pltpu.SMEM((slots,), jnp.int32),
            pltpu.SMEM((requests,), jnp.int32),
            pltpu.VMEM(queries.shape, jnp.bfloat16),
            pltpu.VMEM((requests, rows, head_dim), jnp.bfloat16),
            pltpu.VMEM((slots, page_tokens, head_dim), jnp.bfloat16),
            pltpu.VMEM((slots, page_tokens, head_dim), jnp.bfloat16),
            pltpu.VMEM(out_weight.shape, jnp.bfloat16),
            pltpu.VMEM((slots, rows, page_tokens), jnp.float32),
            pltpu.VMEM((slots + 1, rows, head_dim), jnp.float32),
            pltpu.VMEM((requests + 1, rows, head_dim), jnp.float32),
            pltpu.VMEM((slots + 1, rows, head_dim), jnp.float32),
            pltpu.VMEM((slots + 1, rows, head_dim), jnp.float32),
            pltpu.VMEM(owned, jnp.bfloat16),
            pltpu.VMEM((n_ctx, 1, head_dim), jnp.float32),
            pltpu.VMEM(owned, jnp.bfloat16),
            pltpu.VMEM((n_ctx, 1, head_dim), jnp.float32),
            pltpu.VMEM(owned, jnp.bfloat16),
            pltpu.VMEM(shared, jnp.bfloat16),
            pltpu.SemaphoreType.DMA((5,)),
            pltpu.SemaphoreType.DMA((blocks,)),
            pltpu.SemaphoreType.DMA((blocks,)),
        ]
        + [pltpu.SemaphoreType.DMA((n_ctx,))] * 4
        + [pltpu.SemaphoreType.DMA((GROUP,))] * 2
        + [pltpu.SemaphoreType.DMA((n_ctx,))] * 2
        + [pltpu.SemaphoreType.DMA((n_kvh,))] * 2,
        compiler_params=pltpu.CompilerParams(
            collective_id=0, has_side_effects=True, vmem_limit_bytes=60 << 20
        ),
        name="step",
    )(slot_request, slot_page, lengths, queries, keys, values, out_weight)
    return jnp.sum(shares.astype(jnp.float32), axis=0).astype(jnp.bfloat16)


def solution(mesh):
    placed = (
        P(None, None, "kvh"),
        P("ctx", "kvh", None, None),
        P("ctx", "kvh", None, None),
        P("kvh", "ctx"),
        P(),
        P("ctx"),
        P("ctx"),
    )
    return jax.shard_map(
        functools.partial(per_device, mesh.shape["ctx"], mesh.shape["kvh"]),
        mesh=mesh, in_specs=placed, out_specs=P("kvh", "ctx"), check_vma=False,
    )
```

time: 58.9 us -> 49.7 us (0.84)
  local copies, waits for them, and re-layouts: 7.34 us -> 0 us
  Pallas kernels: 50.7 us -> 48.1 us
  other arithmetic: 0.62 us -> 1.52 us
    unnamed x14 -> x0, local copies, waits for them, and re-layouts: 7.34 us -> none
    pallas_call x2 -> x1, Pallas kernels: 50.7 us -> 48.1 us  [per_device(): pl.pallas_call(functools.partial(step, n_ctx, n_kvh, block), out_shape=ja...]
    reduce_sum x1, other arithmetic: 0.62 us -> 1.52 us  [per_device(): return jnp.sum(shares.astype(jnp.float32), axis=0).astype(jnp.bfloat16)]
where the time goes in v2:
time: 49.7 us; the launch traced here: 49.6 us
  Pallas kernels  48.1 us (97%)
  other arithmetic  1.52 us (3%)
    pallas_call x1, Pallas kernels, per_device(): pl.pallas_call(functools.partial(step, n_ctx, n_kvh, block), out_shape=ja...  48.1 us
    reduce_sum x1, other arithmetic, per_device(): return jnp.sum(shares.astype(jnp.float32), axis=0).astype(jnp.bfloat16)  1.52 us

profile of v2, /device:TPU:1, one launch (start us, length us, event | category | flops | bytes accessed | tf_op | source)
XLA Modules:
  0.0 49.6 jit_solution(17743143682296905488)
XLA Ops:
  0.0 48.1 %step.1 = bf16[8,24,256]{2,1,0:T(8,128)(2,1)} custom-call(s32[64]{0:T(128)} %request_hbm.1, s32[64]{0:T(128)} %page_hbm.1, s32[12]{0:T(128)} %length_hbm.1, bf16[12,16,1024]{2,1,0:T(8,128)(2,1)} %q_hbm.1, bf16[64,1,256,128]{3,2,1,0:T(8,128)(2,1)} %k_hbm.1, bf16[64,1,256,128]{3,2,1,0:T(8,128)(2,1)} %v_hbm.1, bf16[1024,256]{1,0:T(8,128)(2,1)} %w_hbm.1), custom_call_target="tpu_custom_call" | custom-call | tf_op jit(solution)/shard_map/step/pallas_call | solution.py:300
  48.1 1.5 %reduce_sum.12 = bf16[24,256]{1,0:T(8,128)(2,1)} reduce(bf16[8,24,256]{2,1,0:T(8,128)(2,1)} %step.1, bf16[]{:T(256)} %constant.2.clone.1), dimensions={0}, to_apply=%region_0.0 | reduce | flops 43008 | bytes 110594 | tf_op jit(solution)/shard_map/reduce_sum | solution.py:340

commit v3 on v2

--- a/solution.py
+++ b/solution.py
@@ -21,9 +21,9 @@
 def step(
     n_ctx, n_kvh, block,
     request_hbm, page_hbm, length_hbm, q_hbm, k_hbm, v_hbm, w_hbm, out_ref,
-    request_ref, page_ref, length_ref, before_ref, last_ref,
-    q_in, q_rows, k_buf, v_buf, w_buf, s_buf, lane_max, row_max, mass, acc,
-    o_out, stat_out, o_in, stat_in, att, share,
+    request_ref, page_ref, length_ref, last_ref,
+    q_in, q_rows, k_buf, v_buf, w_buf, ahead, top, mass, acc,
+    o_out, stat_out, o_in, stat_in, att, share, share_in,
     small_sem, k_sem, v_sem, o_send, o_recv, t_send, t_recv, z_send, z_recv, x_send, x_recv, p_send, p_recv,
 ):
     c = lax.axis_index("ctx")
@@ -59,7 +59,6 @@
         copy.start()
     for b in range(blocks):
         k_copy(b).start()
-    for b in range(blocks):
         v_copy(b).start()
     w_copy.start()
 
@@ -82,11 +81,11 @@
     lax.fori_loop(1, n_ctx, greet_ctx, 0)
     lax.fori_loop(1, n_kvh, greet_kvh, 0)
 
-    lane_max[slots] = jnp.full((rows, head_dim), FLOOR, jnp.float32)
-    mass[slots] = jnp.zeros((rows, head_dim), jnp.float32)
-    acc[slots] = jnp.zeros((rows, head_dim), jnp.float32)
-    ahead = lax.broadcasted_iota(jnp.int32, (tokens, page_tokens), 1) - lax.broadcasted_iota(
-        jnp.int32, (tokens, page_tokens), 0
+    top[slots] = jnp.full((1, rows), FLOOR, jnp.float32)
+    mass[slots] = jnp.zeros((1, rows), jnp.float32)
+    acc[slots] = jnp.zeros((head_dim, rows), jnp.float32)
+    ahead[...] = lax.broadcasted_iota(jnp.int32, (page_tokens, rows), 0) - lax.rem(
+        lax.broadcasted_iota(jnp.int32, (page_tokens, rows), 1), tokens
     )
     for copy in first:
         copy.wait()
@@ -94,10 +93,12 @@
         for h in range(heads):
             q_rows[r, h * tokens:(h + 1) * tokens, :] = q_in[r, :, h * head_dim:(h + 1) * head_dim]
 
-    def score(b, last):
+    def visit(b, last):
         k_copy(b).wait()
-        for u in range(block):
-            slot = b * block + u
+        v_copy(b).wait()
+        part = [b * block + u for u in range(block)]
+        befores, scores, peaks, masses, outs = [], [], [], [], []
+        for slot in part:
             r = request_ref[slot]
             known = jnp.minimum(r, requests - 1)
             limit = length_ref[known] - tokens - page_ref[slot] * page_tokens
@@ -106,40 +107,33 @@
             for n in range(requests):
                 before = jnp.where(r == n, last[n], before)
             last = tuple(jnp.where(r == n, slot, last[n]) for n in range(requests))
-            before_ref[slot] = before
+            befores.append(before)
             s = lax.dot_general(
-                q_rows[known], k_buf[slot], (((1,), (1,)), ((), ())), preferred_element_type=jnp.float32
+                k_buf[slot], q_rows[known], (((1,), (1,)), ((), ())), preferred_element_type=jnp.float32
             )
-            visible = ahead <= limit
-            for h in range(heads):
-                at = slice(h * tokens, (h + 1) * tokens)
-                masked = jnp.where(visible, s[at], MASKED)
-                s_buf[slot, at, :] = masked
-                folded = jnp.maximum(masked[:, :head_dim], masked[:, head_dim:])
-                lane_max[slot, at, :] = jnp.maximum(lane_max[before, at, :], folded)
+            s = jnp.where(ahead[...] <= limit, s, MASKED)
+            scores.append(s)
+            peaks.append(jnp.maximum(jnp.max(s, axis=0, keepdims=True), FLOOR))
+        for slot, s, peak in zip(part, scores, peaks):
+            weights = jnp.exp2((s - peak) * scale2)
+            masses.append(jnp.sum(weights, axis=0, keepdims=True))
+            outs.append(lax.dot_general(
+                v_buf[slot], weights.astype(jnp.bfloat16), (((0,), (0,)), ((), ())),
+                preferred_element_type=jnp.float32,
+            ))
+        for slot, before, peak, page_mass, page_out in zip(part, befores, peaks, masses, outs):
+            old = top[before]
+            new = jnp.maximum(old, peak)
+            keep = jnp.exp2((old - new) * scale2)
+            gain = jnp.exp2((peak - new) * scale2)
+            top[slot] = new
+            mass[slot] = mass[before] * keep + page_mass * gain
+            acc[slot] = acc[before] * keep + page_out * gain
         return last
 
-    last = lax.fori_loop(0, blocks, score, (jnp.int32(slots),) * requests)
-
+    last = lax.fori_loop(0, blocks, visit, (jnp.int32(slots),) * requests)
     for r in range(requests):
         last_ref[r] = last[r]
-        row_max[r] = jnp.broadcast_to(jnp.max(lane_max[last[r]], axis=1, keepdims=True), (rows, head_dim))
-    row_max[requests] = jnp.zeros((rows, head_dim), jnp.float32)
-
-    def weigh(b, carry):
-        v_copy(b).wait()
-        for u in range(block):
-            slot = b * block + u
-            before = before_ref[slot]
-            reference = row_max[request_ref[slot]]
-            left = jnp.exp2((s_buf[slot, :, :head_dim] - reference) * scale2)
-            right = jnp.exp2((s_buf[slot, :, head_dim:] - reference) * scale2)
-            mass[slot] = mass[before] + (left + right)
-            weights = jnp.concatenate([left, right], axis=1).astype(jnp.bfloat16)
-            acc[slot] = acc[before] + jnp.dot(weights, v_buf[slot], preferred_element_type=jnp.float32)
-        return carry
-
-    lax.fori_loop(0, blocks, weigh, 0)
 
     def stat_copy(j, i):
         device, n = ctx_device(j, i), j * heads + i
@@ -170,34 +164,31 @@
 
     def share_copy(i):
         return pltpu.make_async_remote_copy(
-            src_ref=share.at[kvh_device(i)], dst_ref=out_ref.at[k], send_sem=p_send.at[i], recv_sem=p_recv.at[i],
+            src_ref=share.at[kvh_device(i)], dst_ref=share_in.at[k], send_sem=p_send.at[i], recv_sem=p_recv.at[i],
             device_id=(c, kvh_device(i)), device_id_type=MESH,
         )
 
     pl.semaphore_wait(barrier, n_ctx + n_kvh - 2)
 
-    lane = lax.broadcasted_iota(jnp.int32, (rows, head_dim), 1)
-    row = lax.broadcasted_iota(jnp.int32, (rows, head_dim), 0)
-    diagonal = lane % tokens == row % tokens
-    piece = lane // tokens
+    lane = lax.broadcasted_iota(jnp.int32, (8, rows), 1)
+    kind = lax.broadcasted_iota(jnp.int32, (8, rows), 0)
 
     def hand_out(n, carry):
         j = groups - 1 - n
         a = lax.rem(x + j, groups)
-        packed = jnp.zeros((rows, head_dim), jnp.float32)
+        packed = jnp.zeros((8, rows), jnp.float32)
         for i in range(per_owner):
-            r = a * per_owner + i
-            entry = last_ref[r]
-            total = jnp.sum(mass[entry], axis=1, keepdims=True)
-            packed = jnp.where(piece == i, row_max[r], packed)
-            packed = jnp.where(piece == per_owner + i, jnp.broadcast_to(total, (rows, head_dim)), packed)
+            entry = last_ref[a * per_owner + i]
+            packed = jnp.where(kind == i, top[entry], packed)
+            packed = jnp.where(kind == per_owner + i, mass[entry], packed)
+            turned = acc[entry].T.astype(jnp.bfloat16)
             for h in range(heads):
-                at = slice(h * tokens, (h + 1) * tokens)
-                o_out[a * heads + h, i] = acc[entry, at, :].astype(jnp.bfloat16)
-        packed = jnp.where(diagonal, packed, 0.0)
+                o_out[a * heads + h, i] = turned[h * tokens:(h + 1) * tokens]
+        slanted = pltpu.roll(packed, 0, 1, stride=tokens, stride_axis=0)
         for h in range(heads):
-            at = slice(h * tokens, (h + 1) * tokens)
-            stat_out[a * heads + h] = jnp.sum(packed[at], axis=0, keepdims=True)
+            moved = pltpu.roll(slanted, (rows - h * tokens) % rows, 1)
+            moved = jnp.where(lane // tokens == kind, moved, 0.0)
+            stat_out[a * heads + h] = jnp.sum(moved, axis=0, keepdims=True)
 
         def start(i, inner):
             stat_copy(j, i).start()
@@ -271,7 +262,7 @@
         return carry
 
     lax.fori_loop(1, n_kvh, start_share, 0)
-    out_ref[k] = share[k]
+    share_in[k] = share[k]
 
     def settle(j, i):
         stat_copy(j, i).wait_send()
@@ -284,6 +275,10 @@
         for j in beside:
             x_copy(j, i).wait_send()
     lax.fori_loop(1, n_kvh, finish_share, 0)
+    summed = share_in[0].astype(jnp.float32)
+    for d in range(1, n_kvh):
+        summed += share_in[d].astype(jnp.float32)
+    out_ref[...] = summed.astype(jnp.bfloat16)
 
 
 def per_device(n_ctx, n_kvh, queries, keys, values, out_weight, lengths, slot_request, slot_page):
@@ -294,35 +289,34 @@
     owned = (n_ctx, per_owner, DRAFT_TOKENS, head_dim)
     total_rows = requests * DRAFT_TOKENS
     columns = out_weight.shape[1]
-    block = 4
+    block = 16
     blocks = slots // block
     shared = (n_kvh, total_rows // n_kvh, columns)
-    shares = pl.pallas_call(
+    return pl.pallas_call(
         functools.partial(step, n_ctx, n_kvh, block),
-        out_shape=jax.ShapeDtypeStruct(shared, jnp.bfloat16),
+        out_shape=jax.ShapeDtypeStruct(shared[1:], jnp.bfloat16),
         in_specs=[pl.BlockSpec(memory_space=pltpu.HBM)] * 7,
         out_specs=pl.BlockSpec(memory_space=pltpu.VMEM),
         scratch_shapes=[
             pltpu.SMEM((slots,), jnp.int32),
             pltpu.SMEM((slots,), jnp.int32),
             pltpu.SMEM((requests,), jnp.int32),
-            pltpu.SMEM((slots,), jnp.int32),
             pltpu.SMEM((requests,), jnp.int32),
             pltpu.VMEM(queries.shape, jnp.bfloat16),
             pltpu.VMEM((requests, rows, head_dim), jnp.bfloat16),
             pltpu.VMEM((slots, page_tokens, head_dim), jnp.bfloat16),
             pltpu.VMEM((slots, page_tokens, head_dim), jnp.bfloat16),
             pltpu.VMEM(out_weight.shape, jnp.bfloat16),
-            pltpu.VMEM((slots, rows, page_tokens), jnp.float32),
-            pltpu.VMEM((slots + 1, rows, head_dim), jnp.float32),
-            pltpu.VMEM((requests + 1, rows, head_dim), jnp.float32),
-            pltpu.VMEM((slots + 1, rows, head_dim), jnp.float32),
-            pltpu.VMEM((slots + 1, rows, head_dim), jnp.float32),
+            pltpu.VMEM((page_tokens, rows), jnp.int32),
+            pltpu.VMEM((slots + 1, 1, rows), jnp.float32),
+            pltpu.VMEM((slots + 1, 1, rows), jnp.float32),
+            pltpu.VMEM((slots + 1, head_dim, rows), jnp.float32),
             pltpu.VMEM(owned, jnp.bfloat16),
             pltpu.VMEM((n_ctx, 1, head_dim), jnp.float32),
             pltpu.VMEM(owned, jnp.bfloat16),
             pltpu.VMEM((n_ctx, 1, head_dim), jnp.float32),
             pltpu.VMEM(owned, jnp.bfloat16),
+            pltpu.VMEM(shared, jnp.bfloat16),
             pltpu.VMEM(shared, jnp.bfloat16),
             pltpu.SemaphoreType.DMA((5,)),
             pltpu.SemaphoreType.DMA((blocks,)),
@@ -337,7 +331,6 @@
         ),
         name="step",
     )(slot_request, slot_page, lengths, queries, keys, values, out_weight)
-    return jnp.sum(shares.astype(jnp.float32), axis=0).astype(jnp.bfloat16)
 
 
 def solution(mesh):

time: 49.7 us -> 44.5 us (0.90)
  Pallas kernels: 48.1 us -> 43 us
  other arithmetic: 1.52 us -> 0 us
  local copies, waits for them, and re-layouts: 0 us -> 1.31 us
    pallas_call x1, Pallas kernels: 48.1 us -> 43 us  [per_device(): pl.pallas_call(functools.partial(step, n_ctx, n_kvh, block), out_shape=ja...]
    reduce_sum x1 -> x0, other arithmetic: 1.52 us -> none  [per_device(): return jnp.sum(shares.astype(jnp.float32), axis=0).astype(jnp.bfloat16)]
    unnamed x0 -> x1, local copies, waits for them, and re-layouts: none -> 1.31 us
where the time goes in v3:
time: 44.5 us; the launch traced here: 44.3 us
  Pallas kernels  43 us (97%)
  local copies, waits for them, and re-layouts  1.31 us (3%)
    pallas_call x1, Pallas kernels, per_device(): pl.pallas_call(functools.partial(step, n_ctx, n_kvh, block), out_shape=ja...  43 us
    unnamed x1, local copies, waits for them, and re-layouts  1.31 us

profile of v3, /device:TPU:1, one launch (start us, length us, event | category | flops | bytes accessed | tf_op | source)
XLA Modules:
  0.0 44.3 jit_solution(10895596810629184493)
XLA Ops:
  0.0 43.0 %step.1 = bf16[24,256]{1,0:T(8,128)(2,1)} custom-call(s32[64]{0:T(128)} %request_hbm.1, s32[64]{0:T(128)} %page_hbm.1, s32[12]{0:T(128)} %length_hbm.1, bf16[12,16,1024]{2,1,0:T(8,128)(2,1)} %q_hbm.1, bf16[64,1,256,128]{3,2,1,0:T(8,128)(2,1)} %k_hbm.1, bf16[64,1,256,128]{3,2,1,0:T(8,128)(2,1)} %v_hbm.1, bf16[1024,256]{1,0:T(8,128)(2,1)} %w_hbm.1), custom_call_target="tpu_custom_call" | custom-call | tf_op jit(solution)/shard_map/step/pallas_call | solution.py:295
  43.0 1.3 %copy.9 = bf16[24,256]{1,0:T(8,128)(2,1)} copy(bf16[24,256]{1,0:T(8,128)(2,1)} %step.1) | data formatting | bytes 24576

commit v4 on v3

--- a/solution.py
+++ b/solution.py
@@ -236,32 +236,33 @@
         z_copy(i).wait_recv()
         for j in beside:
             x_copy(j, i).start()
-    for i in [0] + near_first:
-        for j in beside:
+    w_copy.wait()
+    part = share.shape[1]
+    per_group = span // part
+
+    def project(j):
+        a = lax.rem(x + groups - j, groups)
+        operand = jnp.concatenate([att[a * heads + h].reshape(span, head_dim) for h in range(heads)], axis=1)
+        product = jnp.dot(operand, w_buf[...], preferred_element_type=jnp.float32).astype(jnp.bfloat16)
+        for d in range(per_group):
+            share[a * per_group + d] = product[d * part:(d + 1) * part]
+        for d in range(per_group):
+            target = a * per_group + d
+
+            @pl.when(target != k)
+            def _(target=target):
+                share_copy(lax.rem(target + n_kvh - k, n_kvh)).start()
+
+    project(0)
+    for j in beside:
+        for i in [0] + near_first:
             x_copy(j, i).wait_recv()
-
-    w_copy.wait()
-    operand = jnp.concatenate(
-        [
-            jnp.concatenate([att[a * heads + h].reshape(span, head_dim) for a in range(groups)], axis=0)
-            for h in range(heads)
-        ],
-        axis=1,
-    )
-    product = jnp.dot(operand, w_buf[...], preferred_element_type=jnp.float32).astype(jnp.bfloat16)
-    part = share.shape[1]
-    for d in range(n_kvh):
-        share[d] = product[d * part:(d + 1) * part]
-
-    def start_share(i, carry):
-        share_copy(i).start()
-        return carry
+        project(j)
 
     def finish_share(i, carry):
         share_copy(i).wait()
         return carry
 
-    lax.fori_loop(1, n_kvh, start_share, 0)
     share_in[k] = share[k]
 
     def settle(j, i):
@@ -289,7 +290,7 @@
     owned = (n_ctx, per_owner, DRAFT_TOKENS, head_dim)
     total_rows = requests * DRAFT_TOKENS
     columns = out_weight.shape[1]
-    block = 16
+    block = 32
     blocks = slots // block
     shared = (n_kvh, total_rows // n_kvh, columns)
     return pl.pallas_call(

time: 44.5 us -> 42.2 us (0.948)
  the two profiles are of different devices: /device:TPU:1 before, /device:TPU:9 now
where the time goes in v4:
time: 42.2 us; the launch traced here: 42 us
  Pallas kernels  40.7 us (96%)
  local copies, waits for them, and re-layouts  1.31 us (3%)
    pallas_call x1, Pallas kernels, per_device(): pl.pallas_call(functools.partial(step, n_ctx, n_kvh, block), out_shape=ja...  40.7 us
    unnamed x1, local copies, waits for them, and re-layouts  1.31 us

profile of v4, /device:TPU:9, one launch (start us, length us, event | category | flops | bytes accessed | tf_op | source)
XLA Modules:
  0.0 42.0 jit_solution(948081256944981046)
XLA Ops:
  0.0 40.7 %step.1 = bf16[24,256]{1,0:T(8,128)(2,1)} custom-call(s32[64]{0:T(128)} %request_hbm.1, s32[64]{0:T(128)} %page_hbm.1, s32[12]{0:T(128)} %length_hbm.1, bf16[12,16,1024]{2,1,0:T(8,128)(2,1)} %q_hbm.1, bf16[64,1,256,128]{3,2,1,0:T(8,128)(2,1)} %k_hbm.1, bf16[64,1,256,128]{3,2,1,0:T(8,128)(2,1)} %v_hbm.1, bf16[1024,256]{1,0:T(8,128)(2,1)} %w_hbm.1), custom_call_target="tpu_custom_call" | custom-call | tf_op jit(solution)/shard_map/step/pallas_call | solution.py:296
  40.7 1.3 %copy.9 = bf16[24,256]{1,0:T(8,128)(2,1)} copy(bf16[24,256]{1,0:T(8,128)(2,1)} %step.1) | data formatting | bytes 24576

commit v5 on v4

--- a/solution.py
+++ b/solution.py
@@ -95,7 +95,6 @@
 
     def visit(b, last):
         k_copy(b).wait()
-        v_copy(b).wait()
         part = [b * block + u for u in range(block)]
         befores, scores, peaks, masses, outs = [], [], [], [], []
         for slot in part:
@@ -114,6 +113,7 @@
             s = jnp.where(ahead[...] <= limit, s, MASKED)
             scores.append(s)
             peaks.append(jnp.maximum(jnp.max(s, axis=0, keepdims=True), FLOOR))
+        v_copy(b).wait()
         for slot, s, peak in zip(part, scores, peaks):
             weights = jnp.exp2((s - peak) * scale2)
             masses.append(jnp.sum(weights, axis=0, keepdims=True))

time: 42.2 us -> 40.8 us (0.967)
  Pallas kernels: 40.7 us -> 39.4 us
    pallas_call x1, Pallas kernels: 40.7 us -> 39.4 us  [per_device(): pl.pallas_call(functools.partial(step, n_ctx, n_kvh, block), out_shape=ja...]
where the time goes in v5:
time: 40.8 us; the launch traced here: 40.7 us
  Pallas kernels  39.4 us (97%)
  local copies, waits for them, and re-layouts  1.31 us (3%)
    pallas_call x1, Pallas kernels, per_device(): pl.pallas_call(functools.partial(step, n_ctx, n_kvh, block), out_shape=ja...  39.4 us
    unnamed x1, local copies, waits for them, and re-layouts  1.31 us

profile of v5, /device:TPU:9, one launch (start us, length us, event | category | flops | bytes accessed | tf_op | source)
XLA Modules:
  0.0 40.7 jit_solution(2030068954927476344)
XLA Ops:
  0.0 39.4 %step.1 = bf16[24,256]{1,0:T(8,128)(2,1)} custom-call(s32[64]{0:T(128)} %request_hbm.1, s32[64]{0:T(128)} %page_hbm.1, s32[12]{0:T(128)} %length_hbm.1, bf16[12,16,1024]{2,1,0:T(8,128)(2,1)} %q_hbm.1, bf16[64,1,256,128]{3,2,1,0:T(8,128)(2,1)} %k_hbm.1, bf16[64,1,256,128]{3,2,1,0:T(8,128)(2,1)} %v_hbm.1, bf16[1024,256]{1,0:T(8,128)(2,1)} %w_hbm.1), custom_call_target="tpu_custom_call" | custom-call | tf_op jit(solution)/shard_map/step/pallas_call | solution.py:296
  39.4 1.3 %copy.9 = bf16[24,256]{1,0:T(8,128)(2,1)} copy(bf16[24,256]{1,0:T(8,128)(2,1)} %step.1) | data formatting | bytes 24576

commit v6 on v5

--- a/solution.py
+++ b/solution.py
@@ -33,7 +33,9 @@
     per_owner, tokens = o_out.shape[1:3]
     heads = rows // tokens
     groups = n_ctx // heads
-    blocks = slots // block
+    sizes = [16, 48]
+    starts = [sum(sizes[:b]) for b in range(len(sizes))]
+    blocks = len(sizes)
     scale2 = math.log2(math.e) / math.sqrt(head_dim)
     x, z = c // heads, lax.rem(c, heads)
 
@@ -41,11 +43,11 @@
         return pltpu.make_async_copy(source, target, sem)
 
     def k_copy(b):
-        part = pl.ds(b * block, block)
+        part = pl.ds(starts[b], sizes[b])
         return fetch(k_hbm.at[part, 0], k_buf.at[part], k_sem.at[b])
 
     def v_copy(b):
-        part = pl.ds(b * block, block)
+        part = pl.ds(starts[b], sizes[b])
         return fetch(v_hbm.at[part, 0], v_buf.at[part], v_sem.at[b])
 
     first = [
@@ -95,7 +97,7 @@
 
     def visit(b, last):
         k_copy(b).wait()
-        part = [b * block + u for u in range(block)]
+        part = [starts[b] + u for u in range(sizes[b])]
         befores, scores, peaks, masses, outs = [], [], [], [], []
         for slot in part:
             r = request_ref[slot]
@@ -131,7 +133,9 @@
             acc[slot] = acc[before] * keep + page_out * gain
         return last
 
-    last = lax.fori_loop(0, blocks, visit, (jnp.int32(slots),) * requests)
+    last = (jnp.int32(slots),) * requests
+    for b in range(blocks):
+        last = visit(b, last)
     for r in range(requests):
         last_ref[r] = last[r]
 
@@ -230,11 +234,11 @@
     beside = [1, groups - 1] + list(range(2, groups - 1))
     for i in near_first:
         z_copy(i).start()
-    for j in beside:
+    for j in reversed(beside):
         x_copy(j, 0).start()
     for i in near_first:
         z_copy(i).wait_recv()
-        for j in beside:
+        for j in reversed(beside):
             x_copy(j, i).start()
     w_copy.wait()
     part = share.shape[1]
@@ -291,7 +295,7 @@
     total_rows = requests * DRAFT_TOKENS
     columns = out_weight.shape[1]
     block = 32
-    blocks = slots // block
+    blocks = 4
     shared = (n_kvh, total_rows // n_kvh, columns)
     return pl.pallas_call(
         functools.partial(step, n_ctx, n_kvh, block),

time: 40.8 us -> 40.5 us (level)
  the two profiles are of different devices: /device:TPU:9 before, /device:TPU:3 now
where the time goes in v6:
time: 40.5 us; the launch traced here: 40.3 us
  Pallas kernels  39 us (96%)
  local copies, waits for them, and re-layouts  1.31 us (3%)
    pallas_call x1, Pallas kernels, per_device(): pl.pallas_call(functools.partial(step, n_ctx, n_kvh, block), out_shape=ja...  39 us
    unnamed x1, local copies, waits for them, and re-layouts  1.31 us

profile of v6, /device:TPU:3, one launch (start us, length us, event | category | flops | bytes accessed | tf_op | source)
XLA Modules:
  0.0 40.3 jit_solution(12928713437674122929)
XLA Ops:
  0.0 39.0 %step.1 = bf16[24,256]{1,0:T(8,128)(2,1)} custom-call(s32[64]{0:T(128)} %request_hbm.1, s32[64]{0:T(128)} %page_hbm.1, s32[12]{0:T(128)} %length_hbm.1, bf16[12,16,1024]{2,1,0:T(8,128)(2,1)} %q_hbm.1, bf16[64,1,256,128]{3,2,1,0:T(8,128)(2,1)} %k_hbm.1, bf16[64,1,256,128]{3,2,1,0:T(8,128)(2,1)} %v_hbm.1, bf16[1024,256]{1,0:T(8,128)(2,1)} %w_hbm.1), custom_call_target="tpu_custom_call" | custom-call | tf_op jit(solution)/shard_map/step/pallas_call | solution.py:300
  39.0 1.3 %copy.9 = bf16[24,256]{1,0:T(8,128)(2,1)} copy(bf16[24,256]{1,0:T(8,128)(2,1)} %step.1) | data formatting | bytes 24576
